TPU v7x, 128 devices: a whole 4x4x4 slice. The times are simulated.
128 devices in a mesh: frag: 4 (over y_hi, core), aux: 16 (over z, x), orb: 2 (over y_lo).
Axes of the slice: x: 4, y: 4 (y_hi: 2, y_lo: 2; y = y_hi * 2 + y_lo), z: 4, core: 2. Of those that a mesh axis runs over, the one named last changes fastest.
Arguments:
- density: bfloat16 [16384, 2, 8192], P('frag', 'orb', 'aux'), may hold values from -0.046875 to 0.046875
- bath: bfloat16 [16, 2, 8192, 128], P('frag', 'orb', 'aux'), may hold values from -1 to 1
- factor: bfloat16 [16384, 16384], P('orb', 'aux'), may hold values from -6 to 6
- frag_index: int32 [16, 128], replicated, may hold values from 0 to 16383, as said below
- nfrag: int32 [16], replicated, may hold values from 1 to 128
- nbath: int32 [16], replicated, may hold values from 1 to 128
Outputs:
- projected: bfloat16 [16, 256, 16384], P('frag', 'orb', 'aux')
Inputs may be any that keep to these rules, and one draw needn't show every extreme that they name: `frag_index`: the 128 entries of one fragment's row are distinct basis functions; entries at or past nfrag are not read.
All inputs are finite; a program needn't handle non-finite values.
Results may differ from a plain program's by a relative error of at most 0.0049.
Values may be sent and summed in bfloat16 or wider, within the bound.
A program may use at most 128 MiB of HBM per device.

v0:
```python
import functools

import jax
import jax.numpy as jnp
from jax import lax
from jax.experimental import pallas as pl
from jax.experimental.pallas import tpu as pltpu
from jax.sharding import PartitionSpec as P

HIGH = lax.Precision.HIGHEST
MESH = pl.DeviceIdType.MESH
BLOCK = 64
SUB = 8
LANES = 128
SIDE = 4

def spread(value, start, j):
    return jnp.take_along_axis(value, start + j, axis=1)

def invert_tiles(pairs):
    lane = lax.broadcasted_iota(jnp.int32, (SUB, LANES), 1)
    sub = lax.broadcasted_iota(jnp.int32, (SUB, LANES), 0)
    inner = lane % BLOCK
    start = lane - inner
    count = BLOCK // SUB
    pivots = [[None] * count for _ in pairs]
    for now in range(count):
        base = now * SUB
        inside = (inner >= base) & (inner < base + SUB)
        for p, slabs in enumerate(pairs):
            rows = [jnp.broadcast_to(slabs[now][t : t + 1], (SUB, LANES)) for t in range(SUB)]
            entry = [[spread(rows[t], start, base + s) for s in range(t + 1)] for t in range(SUB)]
            rows = [jnp.where(inside, jnp.where(inner == base + t, 1.0, 0.0), rows[t]) for t in range(SUB)]
            inverse, factor = [], {}
            for s in range(SUB):
                inverse.append(1.0 / entry[s][s])
                for t in range(s + 1, SUB):
                    factor[t, s] = entry[t][s] * inverse[s]
                for t in range(s + 1, SUB):
                    for u in range(s + 1, t + 1):
                        entry[t][u] = entry[t][u] - factor[t, s] * entry[u][s]
                for t in range(s + 1, SUB):
                    rows[t] = rows[t] - factor[t, s] * rows[s]
            solved, diag = rows[0], entry[0][0]
            for t in range(1, SUB):
                solved = jnp.where(sub == t, rows[t], solved)
                diag = jnp.where(sub == t, entry[t][t], diag)
            slabs[now] = solved
            pivots[p][now] = diag
            weights = [rows[s] * inverse[s] for s in range(SUB)]
            for s in range(SUB - 1, -1, -1):
                for t in range(s + 1, SUB):
                    weights[s] = weights[s] - factor[t, s] * weights[t]
            for later in range(now + 1, count):
                terms = [spread(slabs[later], start, base + s) * weights[s] for s in range(SUB)]
                while len(terms) > 1:
                    terms = [a + b for a, b in zip(terms[::2], terms[1::2])]
                slabs[later] = jnp.where(inside, 0.0, slabs[later]) - terms[0]
    for p, slabs in enumerate(pairs):
        for now in range(count):
            unit = jnp.where(inner < sub + now * SUB, slabs[now], jnp.where(inner == sub + now * SUB, 1.0, 0.0))
            slabs[now] = unit * lax.rsqrt(pivots[p][now])


def inverse_factor(work_ref, tile_ref, frags):
    size = work_ref.shape[1]
    for block in range(size // BLOCK):
        lo, hi = block * BLOCK, (block + 1) * BLOCK
        for i, f in enumerate(frags):
            left = (i % 2) * BLOCK
            tile_ref[i // 2, :, left : left + BLOCK] = work_ref[f, lo:hi, lo:hi]
        pairs = [[tile_ref[p, r : r + SUB, :] for r in range(0, BLOCK, SUB)] for p in range((len(frags) + 1) // 2)]
        invert_tiles(pairs)
        for p, slabs in enumerate(pairs):
            for r, slab in enumerate(slabs):
                tile_ref[p, r * SUB : (r + 1) * SUB, :] = slab
        yield block
        for i, f in enumerate(frags):
            left = (i % 2) * BLOCK
            inverse = tile_ref[i // 2, :, left : left + BLOCK]
            rows = jnp.dot(inverse, work_ref[f, lo:hi, :], precision=HIGH, preferred_element_type=jnp.float32)
            work_ref[f, lo:hi, :] = rows
            work_ref[f, lo:hi, lo:hi] = inverse
            if hi < size:
                below = jnp.transpose(rows)[hi:, :]
                work_ref[f, hi:, lo:hi] = jnp.zeros((size - hi, BLOCK), jnp.float32)
                work_ref[f, hi:, :] -= jnp.dot(
                    below, work_ref[f, lo:hi, :], precision=HIGH, preferred_element_type=jnp.float32
                )
        yield block


def kernel(
    nfrag_ref, nbath_ref, bath_ref, density_ref, index_ref, factor_ref, out_ref,
    initial, held, partial, gram, gram_in, tiles, outgoing, incoming, density, picked, summed, far, shares, index,
    send_sem, recv_sem, load_sem, gram_sem, value_sem, rows_sem, density_sem, share_sem,
):
    frags, depth, nbmax = bath_ref.shape
    local_rows = density.shape[0]
    nfmax = picked.shape[3]
    size = nfmax + nbmax
    piece = depth // 2
    aux, orb = lax.axis_index("aux"), lax.axis_index("orb")
    up, across = aux // SIDE, aux % SIDE

    def device(coord_up, coord_across):
        return {"aux": coord_up * SIDE + coord_across}

    def turn(value, by):
        return lax.rem(value + by + SIDE, SIDE)

    place = [(across, up), (up, across)]

    def neighbour(half, second, by):
        first, other = place[half]
        if second:
            other = turn(other, by)
        else:
            first = turn(first, by)
        return device(other, first) if half == 0 else device(first, other)

    frag = lax.axis_index("frag")
    high, core = frag // 2, frag % 2
    sibling = {"frag": high * 2 + 1 - core}
    opposite = {"frag": (1 - high) * 2 + core}
    ranks = SIDE * SIDE

    def rank(by):
        return lax.rem(aux + by + ranks, ranks)

    barrier = pltpu.get_barrier_semaphore()
    greeted = [{"aux": rank(by)} for by in range(1, ranks)] + [{"orb": 1 - orb}, sibling, opposite]
    for other in greeted:
        pl.semaphore_signal(barrier, inc=1, device_id=other, device_id_type=MESH)
    partner = {"orb": 1 - orb}
    fetch = pltpu.make_async_copy(density_ref, density, density_sem)
    fetch.start()

    units = [("bath", 0), ("bath", 1), ("rows", 0), ("rows", 1), ("bath", 2), ("rows", 2), ("bath", 3), ("rows", 3)]

    def span(unit):
        kind, f = units[unit]
        return f, (0 if kind == "rows" else nfmax), (nfmax if kind == "rows" else nbmax)

    def put(half, f, low, value):
        first, other = place[half]
        column = pl.multiple_of((other * SIDE + first) * piece, piece)
        initial[half, f, low : low + value.shape[0], pl.ds(column, piece)] = value

    def put_bath(f):
        for half in range(2):
            put(half, f, nfmax, jnp.transpose(bath_ref[f, half * piece : (half + 1) * piece, :]))

    column_index = jnp.transpose(index_ref[...].astype(jnp.float32))
    for f in range(frags):
        for place_of, group in enumerate((0, 2, 1, 3)):
            low = place_of * nfmax
            value = column_index[:, group * frags + f : group * frags + f + 1]
            index[f, low : low + nfmax, :] = jnp.broadcast_to(value, (nfmax, LANES)).astype(jnp.int32)
    for f in range(frags):
        put_bath(f)

    loads = []
    for half in range(2):
        for slot in range(SIDE * SIDE):
            other, first = slot // SIDE, slot % SIDE
            source = slot if half == 0 else first * SIDE + other
            loads.append(
                pltpu.make_async_copy(
                    factor_ref.at[source, half], held.at[half, slot], load_sem.at[half, slot]
                )
            )
            loads[-1].start()

    def region(unit, half, second, offset, part):
        f, low, count = span(unit)
        first, other = place[half]
        if part is not None:
            count = count // 2
            low = low + part * count
        if second:
            column, width = turn(other, offset) * SIDE * piece, SIDE * piece
        else:
            column, width = (other * SIDE + turn(first, offset)) * piece, piece
        column = pl.multiple_of(column, piece)
        return initial.at[half, f, low : low + count, pl.ds(column, width)]

    messages = [(0, None, 1), (0, None, -1), (-1, 0, 1), (1, 1, -1)]
    sent = []

    def message(unit, half, second, index):
        offset, part, by = messages[index]
        where = region(unit, half, second, offset, part)
        slot = (4 if second else 0) + index
        return pltpu.make_async_remote_copy(
            src_ref=where,
            dst_ref=where,
            send_sem=send_sem.at[unit, half, slot],
            recv_sem=recv_sem.at[unit, half, slot],
            device_id=neighbour(half, second, by),
            device_id_type=MESH,
        )

    def send(unit, half, second, index):
        copy = message(unit, half, second, index)
        copy.start()
        sent.append(copy)

    def receive(unit, half, second, index):
        offset, part, by = messages[index]
        where = region(unit, half, second, offset - by, part)
        slot = (4 if second else 0) + index
        pltpu.make_async_remote_copy(
            src_ref=where,
            dst_ref=where,
            send_sem=send_sem.at[unit, half, slot],
            recv_sem=recv_sem.at[unit, half, slot],
            device_id=neighbour(half, second, by),
            device_id_type=MESH,
        ).wait_recv()

    passed = set()

    def stage(number, unit):
        if unit >= len(units) or (number, unit) in passed:
            return
        passed.add((number, unit))
        second = number > 2
        for half in range(2):
            if number == 1:
                send(unit, half, False, 0)
                send(unit, half, False, 1)
            elif number in (2, 4):
                receive(unit, half, second, 0)
                send(unit, half, second, 2)
                receive(unit, half, second, 1)
                send(unit, half, second, 3)
            elif number == 3:
                receive(unit, half, False, 2)
                receive(unit, half, False, 3)
                send(unit, half, True, 0)
                send(unit, half, True, 1)
            else:
                receive(unit, half, True, 2)
                receive(unit, half, True, 3)

    def pick(f):
        step = 8 * LANES
        lane = lax.broadcasted_iota(jnp.int32, (index.shape[1], LANES), 1) + frag * local_rows

        def one(block, total):
            start = pl.multiple_of(block * step, step)
            hot = [
                jnp.where(index[f] == lane + (start + part * LANES), 1.0, 0.0).astype(jnp.bfloat16)
                for part in range(8)
            ]
            rows = density[pl.ds(start, step), :]
            return total + jnp.dot(jnp.concatenate(hot, axis=1), rows, preferred_element_type=jnp.float32)

        total = jnp.zeros((index.shape[1], depth), jnp.float32)
        total = lax.fori_loop(0, local_rows // step, one, total)
        picked[f] = total.astype(picked.dtype).reshape(picked.shape[1:])

    def sibling_copy(f):
        return pltpu.make_async_remote_copy(
            src_ref=picked.at[f, 1 - core],
            dst_ref=summed.at[f],
            send_sem=rows_sem.at[0, f],
            recv_sem=rows_sem.at[1, f],
            device_id=sibling,
            device_id_type=MESH,
        )

    def far_copy(f):
        return pltpu.make_async_remote_copy(
            src_ref=summed.at[f, 1 - high],
            dst_ref=far.at[f],
            send_sem=rows_sem.at[2, f],
            recv_sem=rows_sem.at[3, f],
            device_id=opposite,
            device_id_type=MESH,
        )

    def send_picked(f):
        sibling_copy(f).start()

    def add_sibling(f):
        sibling_copy(f).wait()
        summed[f] = summed[f] + picked[f, core]

    def send_far(f):
        far_copy(f).start()

    def take_rows(f):
        far_copy(f).wait()
        value = summed[f, high] + far[f]
        for half in range(2):
            put(half, f, 0, value[:, half * piece : (half + 1) * piece])

    contract = (((1,), (1,)), ((), ()))

    def make_gram(f):
        total = lax.dot_general(initial[0, f], initial[0, f], contract, preferred_element_type=jnp.float32)
        total += lax.dot_general(initial[1, f], initial[1, f], contract, preferred_element_type=jnp.float32)
        gram[f] = total

    def gram_copy(f):
        return pltpu.make_async_remote_copy(
            src_ref=gram.at[f],
            dst_ref=gram_in.at[f],
            send_sem=gram_sem.at[0, f],
            recv_sem=gram_sem.at[1, f],
            device_id=partner,
            device_id_type=MESH,
        )

    share = size // ranks
    early = frags - 1

    def my_share():
        return pl.ds(pl.multiple_of(aux * share, share), share)

    def early_gram():
        total = jnp.zeros((size, size), jnp.float32)
        for half in range(2):
            first, other = place[half]
            column = pl.multiple_of((other * SIDE + first) * piece, piece)
            block = initial[half, early, :, pl.ds(column, piece)]
            total += lax.dot_general(block, block, contract, preferred_element_type=jnp.float32)
        gram[early] = total

    def share_copy(by):
        rows_of = pl.ds(pl.multiple_of(rank(by) * share, share), share)
        return pltpu.make_async_remote_copy(
            src_ref=gram.at[early, rows_of, :],
            dst_ref=shares.at[by],
            send_sem=share_sem.at[0, by],
            recv_sem=share_sem.at[1, by],
            device_id={"aux": rank(by)},
            device_id_type=MESH,
        )

    def share_swap():
        return pltpu.make_async_remote_copy(
            src_ref=shares.at[0],
            dst_ref=shares.at[ranks],
            send_sem=share_sem.at[0, 0],
            recv_sem=share_sem.at[1, 0],
            device_id=partner,
            device_id_type=MESH,
        )

    def total_copy(by, source):
        rows_of = pl.ds(pl.multiple_of(rank(source) * share, share), share)
        return pltpu.make_async_remote_copy(
            src_ref=gram_in.at[early, rows_of, :],
            dst_ref=gram_in.at[early, rows_of, :],
            send_sem=share_sem.at[2, by],
            recv_sem=share_sem.at[3, by],
            device_id={"aux": rank(by)},
            device_id_type=MESH,
        )

    def early_send():
        for by in range(1, ranks):
            share_copy(by).start()

    def early_sum():
        for by in range(1, ranks):
            share_copy(by).wait()
        total = gram[early, my_share(), :]
        for by in range(1, ranks):
            total = total + shares[by]
        shares[0] = total

    def early_swap():
        share_swap().start()

    def early_total():
        share_swap().wait()
        gram_in[early, my_share(), :] = shares[0] + shares[ranks]

    def early_spread():
        for by in range(1, ranks):
            total_copy(by, 0).start()

    def early_take():
        for by in range(1, ranks):
            total_copy(by, 0).wait_send()
            total_copy(by, -by).wait_recv()

    width = 512
    tiles_q = partial.shape[2] // width

    def project(f, low=0, high_row=size, offsets=None):
        count = high_row - low

        def one(q, carry):
            column = pl.ds(pl.multiple_of(q * width, width), width)
            total = jnp.zeros((count, width), jnp.float32)
            if offsets is None:
                def add(half, total):
                    block = held[half, :, :, column].reshape(SIDE * SIDE * piece, width)
                    return total + jnp.dot(
                        initial[half, f, low:high_row], block, preferred_element_type=jnp.float32
                    )

                total = lax.fori_loop(0, 2, add, total)
            for half in range(0 if offsets is None else 2):
                for offset in offsets:
                    start = turn(place[half][1], offset) * SIDE
                    block = held[half, pl.ds(start, SIDE), :, column].reshape(SIDE * piece, width)
                    columns = pl.ds(pl.multiple_of(start * piece, piece), SIDE * piece)
                    total += jnp.dot(initial[half, f, low:high_row, columns], block, preferred_element_type=jnp.float32)
            if offsets is not None and offsets[0] != 0:
                total += partial[f, low:high_row, column]
            partial[f, low:high_row, column] = total
            return carry

        lax.fori_loop(0, tiles_q, one, 0)

    row = lax.broadcasted_iota(jnp.int32, (size, size), 0)
    col = lax.broadcasted_iota(jnp.int32, (size, size), 1)

    def both_live(f):
        fragment = frag * frags + f
        used, used_bath = nfrag_ref[fragment], nbath_ref[fragment] + nfmax
        live_row = (row < used) | ((row >= nfmax) & (row < used_bath))
        live_col = (col < used) | ((col >= nfmax) & (col < used_bath))
        return live_row & live_col

    def prepare(f):
        total = gram_in[f]
        if f != early:
            gram_copy(f).wait()
            total = gram[f] + gram_in[f]
        gram_in[f] = jnp.where(both_live(f), total, jnp.where(row == col, 1.0, 0.0))

    def value_copy(f):
        return pltpu.make_async_remote_copy(
            src_ref=outgoing.at[f],
            dst_ref=incoming.at[f],
            send_sem=value_sem.at[0, f],
            recv_sem=value_sem.at[1, f],
            device_id=partner,
            device_id_type=MESH,
        )

    def mask(f):
        gram_in[f] = jnp.where(both_live(f) & (row >= col), gram_in[f], 0.0)

    def apply(f):
        theirs = gram_in[f, pl.ds(pl.multiple_of((1 - orb) * nfmax, nfmax), nfmax), :]
        mine = gram_in[f, pl.ds(pl.multiple_of(orb * nfmax, nfmax), nfmax), :]
        value = jnp.dot(theirs, partial[f], precision=HIGH, preferred_element_type=jnp.float32)
        outgoing[f] = value.astype(outgoing.dtype)
        value = jnp.dot(mine, partial[f], precision=HIGH, preferred_element_type=jnp.float32)
        value_copy(f).start()
        partial[f, :nfmax, :] = value

    def finish(f):
        value_copy(f).wait()
        out_ref[f] = (partial[f, :nfmax, :] + incoming[f].astype(jnp.float32)).astype(out_ref.dtype)

    pl.semaphore_wait(barrier, len(greeted))
    stage(1, 0)
    stage(1, 1)
    stage(1, 4)
    fetch.wait()
    pick(0)
    stage(2, 0)
    stage(2, 1)
    stage(1, 6)
    send_picked(0)
    pick(2)
    stage(3, 0)
    pick(3)
    pick(1)
    add_sibling(0)
    send_picked(1)
    send_far(0)
    stage(3, 1)
    stage(4, 0)
    take_rows(0)
    send_picked(2)
    add_sibling(1)
    stage(1, 2)
    send_far(1)
    send_picked(3)
    stage(4, 1)
    stage(2, 2)
    take_rows(1)
    for copy in loads:
        copy.wait()
    stage(5, 0)
    stage(1, 3)
    stage(3, 2)
    add_sibling(2)
    stage(5, 1)
    send_far(2)
    add_sibling(3)
    stage(2, 4)
    stage(2, 3)
    send_far(3)
    take_rows(2)
    stage(4, 2)
    stage(3, 3)
    take_rows(3)
    stage(5, 2)
    make_gram(0)
    early_gram()
    project(0, 0, nfmax)
    stage(1, 5)
    stage(4, 3)
    gram_copy(0).start()
    project(1, nfmax, size)
    early_send()
    stage(5, 3)
    stage(2, 5)
    make_gram(1)
    stage(3, 4)
    stage(1, 7)
    gram_copy(1).start()
    stage(3, 5)
    prepare(0)
    project(1, 0, nfmax)
    early_sum()
    prepare(1)
    steps = inverse_factor(gram_in, tiles, [0,1])
    next(steps)
    next(steps)
    next(steps)
    stage(4, 4)
    next(steps)
    early_swap()
    next(steps)
    next(steps)
    stage(4, 5)
    next(steps)
    early_total()
    next(steps)
    stage(2, 6)
    mask(1)
    stage(5, 4)
    project(2, nfmax, size)
    stage(2, 7)
    early_spread()
    stage(5, 5)
    make_gram(2)
    mask(0)
    gram_copy(2).start()
    stage(3, 6)
    apply(1)
    project(0, nfmax, size)
    early_take()
    apply(0)
    prepare(3)
    project(2, 0, nfmax)
    stage(3, 7)
    prepare(2)
    steps = inverse_factor(gram_in, tiles, [2,3])
    next(steps)
    next(steps)
    next(steps)
    next(steps)
    stage(4, 6)
    next(steps)
    next(steps)
    next(steps)
    stage(4, 7)
    next(steps)
    mask(2)
    apply(2)
    project(3, 0, nfmax, (0,))
    project(3, 0, nfmax, (-1,1))
    stage(5, 6)
    stage(5, 7)
    mask(3)
    project(3, nfmax, size)
    project(3, 0, nfmax, (2,))
    apply(3)
    finish(0)
    finish(2)
    finish(1)
    finish(3)
    for copy in sent:
        copy.wait_send()


def fused(nfrag, nbath, bath, density, index, factor):
    frags, depth, nbmax = bath.shape
    local_rows = density.shape[0]
    total_frags, nfmax = index.shape
    groups = total_frags // frags
    size = nfmax + nbmax
    columns = factor.shape[1]
    ranks, piece = SIDE * SIDE, depth // 2
    sems = pltpu.SemaphoreType.DMA
    half_rows = size // 2
    vmem = pltpu.VMEM
    return pl.pallas_call(
        kernel,
        out_shape=jax.ShapeDtypeStruct((frags, half_rows, columns), jnp.bfloat16),
        in_specs=[
            pl.BlockSpec(memory_space=kind)
            for kind in (pltpu.SMEM, pltpu.SMEM, vmem, pl.ANY, vmem, pl.ANY)
        ],
        out_specs=pl.BlockSpec(memory_space=vmem),
        scratch_shapes=[
            vmem((2, frags, size, ranks * piece), jnp.bfloat16),
            vmem((2, ranks, piece, columns), jnp.bfloat16),
            vmem((frags, size, columns), jnp.float32),
            vmem((frags, size, size), jnp.float32),
            vmem((frags, size, size), jnp.float32),
            vmem((2, BLOCK, LANES), jnp.float32),
            vmem((frags, half_rows, columns), jnp.bfloat16),
            vmem((frags, half_rows, columns), jnp.bfloat16),
            vmem((local_rows, depth), jnp.bfloat16),
            vmem((frags, 2, groups // 2, nfmax, depth), jnp.bfloat16),
            vmem((frags, groups // 2, nfmax, depth), jnp.bfloat16),
            vmem((frags, nfmax, depth), jnp.bfloat16),
            vmem((ranks + 1, size // ranks, size), jnp.float32),
            vmem((frags, groups * nfmax, LANES), jnp.int32),
            sems((2 * frags, 2, 8)),
            sems((2 * frags, 2, 8)),
            sems((2, ranks)),
            sems((2, frags)),
            sems((2, frags)),
            sems((4, frags)),
            sems(()),
            sems((4, ranks)),
        ],
        compiler_params=pltpu.CompilerParams(
            collective_id=0, has_side_effects=True, vmem_limit_bytes=63 * 1024 * 1024
        ),
    )(nfrag, nbath, bath, density, index, factor.reshape(ranks, 2, piece, columns))


def per_device(density, bath, factor, frag_index, nfrag, nbath):
    local_rows, _, depth = density.shape
    frags, _, _, nbmax = bath.shape
    return fused(
        nfrag, nbath, bath.reshape(frags, depth, nbmax), density.reshape(local_rows, depth), frag_index, factor
    )


def solution(mesh):
    placed = (
        P("frag", "orb", "aux"),
        P("frag", "orb", "aux", None),
        P("orb", "aux"),
        P(),
        P(),
        P(),
    )
    return jax.shard_map(
        per_device, mesh=mesh, in_specs=placed, out_specs=P("frag", "orb", "aux"), check_vma=False
    )
```

profile of v0, /device:TPU:0, one launch (start us, length us, event | category | flops | bytes accessed | tf_op | source)
XLA Modules:
  0.0 135.8 jit_solution(8611511870720758087)
XLA Ops:
  0.0 133.5 %shard_map.64 = bf16[4,128,1024]{2,1,0:T(8,128)(2,1)} custom-call(s32[16]{0:T(128)} %nfrag_ref.1, s32[16]{0:T(128)} %nbath_ref.1, bf16[4,512,128]{2,1,0:T(8,128)(2,1)} %bitcast.5, bf16[4096,512]{1,0:T(8,128)(2,1)} %bitcast.4, s32[16,128]{1,0:T(8,128)} %index_ref.1, bf16[16,2,256,1024]{3,2,1,0:T(8,128)(2,1)} %bitcast.3), custom_call_target="tpu_custom_call" | custom-call | tf_op jit(solution)/shard_map/pallas_call | solution.py:601
  133.6 2.3 %copy.8 = bf16[4,128,1024]{2,1,0:T(8,128)(2,1)} copy(bf16[4,128,1024]{2,1,0:T(8,128)(2,1)} %shard_map.64) | data formatting | bytes 2097152
where the time goes:
time: 136 us
  Pallas kernels  134 us (99%)
  local copies, waits for them, and re-layouts  2.26 us (2%)
    pallas_call x1, Pallas kernels, fused(): pl.pallas_call(kernel, out_shape=jax.ShapeDtypeStruct((frags, half_rows,...  134 us

commit v1 on v0

--- a/solution.py
+++ b/solution.py
@@ -151,13 +151,15 @@
         for half in range(2):
             put(half, f, nfmax, jnp.transpose(bath_ref[f, half * piece : (half + 1) * piece, :]))
 
-    column_index = jnp.transpose(index_ref[...].astype(jnp.float32))
-    for f in range(frags):
-        for place_of, group in enumerate((0, 2, 1, 3)):
-            low = place_of * nfmax
-            value = column_index[:, group * frags + f : group * frags + f + 1]
-            index[f, low : low + nfmax, :] = jnp.broadcast_to(value, (nfmax, LANES)).astype(jnp.int32)
-    for f in range(frags):
+    def put_index():
+        column_index = jnp.transpose(index_ref[...].astype(jnp.float32))
+        for f in range(frags):
+            for place_of, group in enumerate((0, 2, 1, 3)):
+                low = place_of * nfmax
+                value = column_index[:, group * frags + f : group * frags + f + 1]
+                index[f, low : low + nfmax, :] = jnp.broadcast_to(value, (nfmax, LANES)).astype(jnp.int32)
+
+    for f in range(2):
         put_bath(f)
 
     loads = []
@@ -464,123 +466,126 @@
 
     pl.semaphore_wait(barrier, len(greeted))
     stage(1, 0)
+    put_bath(2)
+    fetch.wait()
+    put_index()
+    stage(1, 4)
+    put_bath(3)
+    stage(2, 0)
     stage(1, 1)
-    stage(1, 4)
-    fetch.wait()
     pick(0)
-    stage(2, 0)
+    stage(3, 0)
+    send_picked(0)
+    pick(1)
     stage(2, 1)
-    stage(1, 6)
-    send_picked(0)
+    send_picked(1)
+    stage(4, 0)
+    add_sibling(0)
+    stage(3, 1)
+    send_far(0)
+    stage(5, 0)
     pick(2)
-    stage(3, 0)
-    pick(3)
-    pick(1)
-    add_sibling(0)
-    send_picked(1)
-    send_far(0)
-    stage(3, 1)
-    stage(4, 0)
     take_rows(0)
+    add_sibling(1)
     send_picked(2)
-    add_sibling(1)
     stage(1, 2)
+    stage(4, 1)
     send_far(1)
-    send_picked(3)
-    stage(4, 1)
-    stage(2, 2)
-    take_rows(1)
     for copy in loads:
         copy.wait()
-    stage(5, 0)
+    pick(3)
+    stage(2, 2)
+    stage(2, 4)
+    stage(3, 2)
+    send_picked(3)
+    take_rows(1)
+    add_sibling(2)
     stage(1, 3)
-    stage(3, 2)
-    add_sibling(2)
+    send_far(2)
+    project(0, nfmax, size)
+    stage(1, 6)
+    stage(2, 3)
+    stage(3, 3)
     stage(5, 1)
-    send_far(2)
     add_sibling(3)
-    stage(2, 4)
-    stage(2, 3)
-    send_far(3)
     take_rows(2)
     stage(4, 2)
-    stage(3, 3)
+    send_far(3)
+    stage(4, 3)
+    stage(1, 5)
     take_rows(3)
     stage(5, 2)
     make_gram(0)
     early_gram()
-    project(0, 0, nfmax)
-    stage(1, 5)
-    stage(4, 3)
     gram_copy(0).start()
-    project(1, nfmax, size)
+    stage(3, 4)
     early_send()
     stage(5, 3)
+    project(0, 0, nfmax)
+    make_gram(1)
     stage(2, 5)
-    make_gram(1)
-    stage(3, 4)
+    gram_copy(1).start()
     stage(1, 7)
-    gram_copy(1).start()
+    project(1, 0, nfmax)
+    prepare(0)
+    project(1, nfmax, size)
+    early_sum()
     stage(3, 5)
-    prepare(0)
-    project(1, 0, nfmax)
-    early_sum()
+    stage(4, 4)
     prepare(1)
     steps = inverse_factor(gram_in, tiles, [0,1])
     next(steps)
     next(steps)
     next(steps)
-    stage(4, 4)
     next(steps)
     early_swap()
     next(steps)
-    next(steps)
     stage(4, 5)
     next(steps)
+    stage(2, 7)
+    next(steps)
+    next(steps)
+    stage(5, 4)
     early_total()
-    next(steps)
     stage(2, 6)
+    stage(5, 5)
+    early_spread()
+    make_gram(2)
+    stage(3, 7)
+    gram_copy(2).start()
+    project(2, nfmax, size)
+    project(2, 0, nfmax)
+    mask(0)
+    early_take()
+    project(3, 0, nfmax, (0,))
     mask(1)
-    stage(5, 4)
-    project(2, nfmax, size)
-    stage(2, 7)
-    early_spread()
-    stage(5, 5)
-    make_gram(2)
-    mask(0)
-    gram_copy(2).start()
     stage(3, 6)
-    apply(1)
-    project(0, nfmax, size)
-    early_take()
+    prepare(3)
     apply(0)
-    prepare(3)
-    project(2, 0, nfmax)
-    stage(3, 7)
     prepare(2)
     steps = inverse_factor(gram_in, tiles, [2,3])
     next(steps)
     next(steps)
+    apply(1)
+    next(steps)
     next(steps)
     next(steps)
     stage(4, 6)
     next(steps)
-    next(steps)
-    next(steps)
     stage(4, 7)
+    next(steps)
     next(steps)
     mask(2)
     apply(2)
-    project(3, 0, nfmax, (0,))
     project(3, 0, nfmax, (-1,1))
     stage(5, 6)
+    project(3, nfmax, size)
     stage(5, 7)
+    project(3, 0, nfmax, (2,))
     mask(3)
-    project(3, nfmax, size)
-    project(3, 0, nfmax, (2,))
     apply(3)
+    finish(2)
     finish(0)
-    finish(2)
     finish(1)
     finish(3)
     for copy in sent:

time: 136 us -> 135 us (level)
  no operation moved by 1% of the time
where the time goes in v1:
time: 135 us
  Pallas kernels  133 us (99%)
  local copies, waits for them, and re-layouts  2.26 us (2%)
    pallas_call x1, Pallas kernels, fused(): pl.pallas_call(kernel, out_shape=jax.ShapeDtypeStruct((frags, half_rows,...  133 us

profile of v1, /device:TPU:0, one launch (start us, length us, event | category | flops | bytes accessed | tf_op | source)
XLA Modules:
  0.0 135.2 jit_solution(3764188761865812052)
XLA Ops:
  0.0 133.0 %shard_map.64 = bf16[4,128,1024]{2,1,0:T(8,128)(2,1)} custom-call(s32[16]{0:T(128)} %nfrag_ref.1, s32[16]{0:T(128)} %nbath_ref.1, bf16[4,512,128]{2,1,0:T(8,128)(2,1)} %bitcast.5, bf16[4096,512]{1,0:T(8,128)(2,1)} %bitcast.4, s32[16,128]{1,0:T(8,128)} %index_ref.1, bf16[16,2,256,1024]{3,2,1,0:T(8,128)(2,1)} %bitcast.3), custom_call_target="tpu_custom_call" | custom-call | tf_op jit(solution)/shard_map/pallas_call | solution.py:606
  133.0 2.3 %copy.8 = bf16[4,128,1024]{2,1,0:T(8,128)(2,1)} copy(bf16[4,128,1024]{2,1,0:T(8,128)(2,1)} %shard_map.64) | data formatting | bytes 2097152

commit v2 on v1

--- a/solution.py
+++ b/solution.py
@@ -394,7 +394,7 @@
     width = 512
     tiles_q = partial.shape[2] // width
 
-    def project(f, low=0, high_row=size, offsets=None):
+    def project(f, low, high_row, offsets=None, unroll=False):
         count = high_row - low
 
         def one(q, carry):
@@ -407,7 +407,7 @@
                         initial[half, f, low:high_row], block, preferred_element_type=jnp.float32
                     )
 
-                total = lax.fori_loop(0, 2, add, total)
+                total = lax.fori_loop(0, 2, add, total, unroll=unroll)
             for half in range(0 if offsets is None else 2):
                 for offset in offsets:
                     start = turn(place[half][1], offset) * SIDE
@@ -526,7 +526,7 @@
     stage(2, 5)
     gram_copy(1).start()
     stage(1, 7)
-    project(1, 0, nfmax)
+    project(1, 0, nfmax, unroll=True)
     prepare(0)
     project(1, nfmax, size)
     early_sum()
@@ -553,8 +553,8 @@
     make_gram(2)
     stage(3, 7)
     gram_copy(2).start()
-    project(2, nfmax, size)
-    project(2, 0, nfmax)
+    project(2, nfmax, size, unroll=True)
+    project(2, 0, nfmax, unroll=True)
     mask(0)
     early_take()
     project(3, 0, nfmax, (0,))
@@ -579,7 +579,7 @@
     apply(2)
     project(3, 0, nfmax, (-1,1))
     stage(5, 6)
-    project(3, nfmax, size)
+    project(3, nfmax, size, unroll=True)
     stage(5, 7)
     project(3, 0, nfmax, (2,))
     mask(3)

time: 135 us -> 134 us (level)
  no operation moved by 1% of the time
where the time goes in v2:
time: 134 us
  Pallas kernels  132 us (99%)
  local copies, waits for them, and re-layouts  2.26 us (2%)
    pallas_call x1, Pallas kernels, fused(): pl.pallas_call(kernel, out_shape=jax.ShapeDtypeStruct((frags, half_rows,...  132 us

profile of v2, /device:TPU:0, one launch (start us, length us, event | category | flops | bytes accessed | tf_op | source)
XLA Modules:
  0.0 134.3 jit_solution(876533758658272478)
XLA Ops:
  0.0 132.0 %shard_map.64 = bf16[4,128,1024]{2,1,0:T(8,128)(2,1)} custom-call(s32[16]{0:T(128)} %nfrag_ref.1, s32[16]{0:T(128)} %nbath_ref.1, bf16[4,512,128]{2,1,0:T(8,128)(2,1)} %bitcast.5, bf16[4096,512]{1,0:T(8,128)(2,1)} %bitcast.4, s32[16,128]{1,0:T(8,128)} %index_ref.1, bf16[16,2,256,1024]{3,2,1,0:T(8,128)(2,1)} %bitcast.3), custom_call_target="tpu_custom_call" | custom-call | tf_op jit(solution)/shard_map/pallas_call | solution.py:606
  132.0 2.3 %copy.8 = bf16[4,128,1024]{2,1,0:T(8,128)(2,1)} copy(bf16[4,128,1024]{2,1,0:T(8,128)(2,1)} %shard_map.64) | data formatting | bytes 2097152
